TPU v7x, 32 devices: a whole 2x2x4 slice. The times are simulated.
32 devices in a mesh: groups: 2 (over x), tiles: 8 (over z, y), seg: 2 (over core).
Axes of the slice: x: 2, y: 2, z: 4, core: 2. Of those that a mesh axis runs over, the one named last changes fastest.
Arguments:
- records: bfloat16 [2, 12800, 2048], P('seg', 'tiles', 'groups'), parts along dimension 2, may hold values from -6 to 6
- channel_live: int32 [2048], P(('groups', 'tiles')), parts along dimension 0, may hold values 0 or 1
Outputs:
- cross_spectra: bfloat16 [2, 2048, 128, 256], P(None, ('groups', 'tiles'), None, 'seg'), parts along dimension 1
There are 2 independent parts, one for each index of `groups`. A program takes and returns all parts, laid end to end along the dimension named above; each array names one. Nothing has to cross between parts.
All inputs are finite; a program needn't handle non-finite values. No bound on the sum of `channel_live` on one device may be relied on, other than what follows from the above.
Results may differ from a plain program's by a relative error of at most 0.0069.
Values may be sent and summed in bfloat16 or wider, within the bound.
A program may use at most 128 MiB of HBM per device.

v0:
```python
import math

import jax
import jax.numpy as jnp
from jax import lax
from jax.sharding import PartitionSpec as P

OFFS = 128
L = 12800
FIRST_BIN = 64
F = 256


epsilon = 1e-06


def from_behind(block, axis, distance):
    devices = range(lax.axis_size(axis))
    route = [(i - distance, i) for i in devices if i - distance in devices]
    return lax.ppermute(block, axis, route)


def band_table(length, first_bin, bin_count):
    sample = jnp.arange(length, dtype=jnp.int32)[:, None]
    bin_index = jnp.arange(bin_count, dtype=jnp.int32)[None, :] + first_bin
    phase_index = sample * bin_index % length
    phase_angle = phase_index.astype(jnp.float32) * (2.0 * math.pi / length)
    hann_taper = 0.5 - 0.5 * jnp.cos(sample.astype(jnp.float32) * (2.0 * math.pi / length))
    return jnp.concatenate(
        [hann_taper * jnp.cos(phase_angle), -hann_taper * jnp.sin(phase_angle)], axis=1
    ).astype(jnp.bfloat16)


def whiten(spectra, live_mask):
    mean_power = jnp.mean(spectra * spectra, axis=2, keepdims=True)
    gains = lax.rsqrt(mean_power + epsilon) * live_mask.astype(jnp.float32)[None, :, None]
    return (spectra * gains).astype(jnp.bfloat16)


def offset_view(wide, offsets):
    window_count, double_rows, bin_width = wide.shape
    group_size = double_rows // 2
    repeated = jnp.broadcast_to(
        wide[:, None], (window_count, group_size + 1, double_rows, bin_width)
    )
    flat_rows = repeated.reshape(window_count, (group_size + 1) * double_rows, bin_width)
    skewed = flat_rows[:, : group_size * (double_rows + 1)].reshape(
        window_count, group_size, double_rows + 1, bin_width
    )
    return skewed[:, :, :offsets]


def cross_band(own_real, own_imag, next_real, next_imag, offsets):
    wide_real = jnp.concatenate([own_real, next_real], axis=1)
    wide_imag = jnp.concatenate([own_imag, next_imag], axis=1)
    moved_real = offset_view(wide_real, offsets).astype(jnp.float32)
    moved_imag = offset_view(wide_imag, offsets).astype(jnp.float32)
    base_real = own_real.astype(jnp.float32)[:, :, None, :]
    base_imag = own_imag.astype(jnp.float32)[:, :, None, :]
    real_sum = jnp.sum(base_real * moved_real + base_imag * moved_imag, axis=0)
    imag_sum = jnp.sum(base_imag * moved_real - base_real * moved_imag, axis=0)
    return jnp.stack([real_sum, imag_sum])


def neighbour(real_part, imag_part):
    return from_behind((real_part, imag_part), "tiles", -1)


def local(records, channel_live):
    basis_table = band_table(L, FIRST_BIN, F)
    local_samples = records.shape[1]
    first_sample = lax.axis_index("tiles") * local_samples
    local_basis = lax.dynamic_slice_in_dim(basis_table, first_sample, local_samples, 0)
    own_rows = lax.psum_scatter(
        jnp.einsum("wnc,nk->cwk", records, local_basis, preferred_element_type=jnp.float32),
        "tiles",
        scatter_dimension=0,
        tiled=True,
    )
    spectra = jnp.transpose(own_rows, (1, 0, 2))
    whitened = whiten(spectra, channel_live)
    real_part = whitened[..., :F]
    imag_part = whitened[..., F:]
    windows = records.shape[0] * lax.axis_size("seg")
    real_all, imag_all = (
        lax.all_to_all(real_part, "seg", split_axis=2, concat_axis=0, tiled=True),
        lax.all_to_all(imag_part, "seg", split_axis=2, concat_axis=0, tiled=True),
    )
    next_real, next_imag = neighbour(real_all, imag_all)
    stacked = cross_band(real_all, imag_all, next_real, next_imag, OFFS)
    return (stacked / windows).astype(jnp.bfloat16)


def solution(mesh):
    in_specs = (P("seg", "tiles", "groups"), P(("groups", "tiles")))
    out_specs = P(None, ("groups", "tiles"), None, "seg")
    return jax.shard_map(local, mesh=mesh, in_specs=in_specs, out_specs=out_specs, check_vma=False)
```

profile of v0, /device:TPU:1, one launch (start us, length us, event | category | flops | bytes accessed | tf_op | source)
XLA Modules:
  0.0 257.8 jit_solution(3358089407634171667)
XLA Ops:
  6.5 0.2 multiply_subtract_fusion
  6.8 61.4 %multiply_convert_fusion = (bf16[12800,256]{1,0:T(8,128)(2,1)S(1)}, bf16[12800,256]{1,0:T(8,128)(2,1)S(1)}) fusion(f32[12800]{0:T(1024)S(1)} %get-tuple-element.12, s32[256]{0:T(256)S(1)} %iota_add_fusion, f32[12800]{0:T(1024)S(1)} %get-tuple-element.11), kind=kLoop, calls=%fused_computation.15 | loop fusion | flops 42598400 | bytes 13210624 | tf_op jit(solution)/shard_map/convert.1
  68.2 0.0 copy-start.2
  68.2 3.4 %fusion.14 = f32[1024,1,512]{0,2,1:T(8,128)} fusion(bf16[1,1600,1024]{2,1,0:T(8,128)(2,1)S(1)} %copy-done, s32[]{:T(128)S(6)} %select_n.13, bf16[12800,256]{1,0:T(8,128)(2,1)S(1)} %get-tuple-element.10, bf16[12800,256]{1,0:T(8,128)(2,1)S(1)} %get-tuple-element.9), kind=kOutput, calls=%fused_computation.24 | convolution fusion | flops 1680998400 | bytes 18481156 | tf_op jit(solution)/shard_map/wnc,nk->cwk/dot_general | solution.py:75
  71.6 0.0 reduce-scatter.2.cloned.1.call-update
  71.6 68.6 %reduce-scatter.2.cloned.1.call-done = f32[128,1,512]{0,2,1:T(8,128)} async-done(((f32[1024,1,512]{0,2,1:T(8,128)}), f32[128,1,512]{0,2,1:T(8,128)}) %reduce-scatter.2.cloned.1.call-update) | async-done | bytes 262160 | tf_op jit(solution)/shard_map/reduce_scatter | solution.py:74
  140.2 1.0 fusion.19
  141.3 1.0 fusion.20
  142.3 0.1 copy.26
  142.4 0.5 broadcast.61
  142.9 1.0 reduce.2
  143.9 5.9 %all_to_all.36 = bf16[2,2,8192]{2,1,0:T(2,128)(2,1)S(1)} all-to-all(bf16[2,2,8192]{2,1,0:T(2,128)(2,1)S(1)} %reshape.109), channel_id=1, replica_groups=mesh['groups'=2,'tiles'=8,'seg'=2] {'seg'}, dimensions={0} | all-to-all | bytes 131072 | tf_op jit(solution)/shard_map/all_to_all | solution.py:86
  149.8 0.1 reshape.110
  149.9 1.3 collective-permute-start
  151.2 0.1 copy.16
  151.3 0.1 copy.25
  151.4 1.0 reduce.1
  152.5 3.8 %all_to_all.37 = bf16[2,2,8192]{2,1,0:T(2,128)(2,1)S(1)} all-to-all(bf16[2,2,8192]{2,1,0:T(2,128)(2,1)S(1)} %reshape.111), channel_id=1, replica_groups=mesh['groups'=2,'tiles'=8,'seg'=2] {'seg'}, dimensions={0} | all-to-all | bytes 131072 | tf_op jit(solution)/shard_map/all_to_all | solution.py:87
  156.3 0.1 reshape.112
  156.3 1.3 collective-permute-start.1
  157.6 0.1 copy.19
  157.8 0.0 collective-permute-done
  157.8 0.1 copy.17
  157.9 4.3 %broadcast_in_dim.4 = bf16[2,129,256,128]{3,2,1,0:T(8,128)(2,1)S(1)} broadcast(bf16[2,256,128]{2,1,0:T(8,128)(2,1)S(1)} %copy.17), dimensions={0,2,3} | broadcast | bytes 17039360 | tf_op jit(solution)/shard_map/broadcast_in_dim | solution.py:43
  162.2 6.6 %slice.25 = bf16[2,32896,128]{2,1,0:T(8,128)(2,1)} slice(bf16[2,33024,128]{2,1,0:T(8,128)(2,1)S(1)} %bitcast.38), slice={[0:2], [0:32896], [0:128]} | slice | bytes 33685504 | tf_op jit(solution)/shard_map/slice | solution.py:47
  168.8 24.5 %reshape.106 = bf16[2,128,257,128]{3,2,1,0:T(8,128)(2,1)} reshape(bf16[2,32896,128]{2,1,0:T(8,128)(2,1)} %slice.25) | data formatting | bytes 33685504 | tf_op jit(solution)/shard_map/reshape | solution.py:47
  193.3 0.1 copy.20
  193.5 4.3 %broadcast_in_dim.5 = bf16[2,129,256,128]{3,2,1,0:T(8,128)(2,1)S(1)} broadcast(bf16[2,256,128]{2,1,0:T(8,128)(2,1)S(1)} %copy.20), dimensions={0,2,3} | broadcast | bytes 17039360 | tf_op jit(solution)/shard_map/broadcast_in_dim | solution.py:43
  197.8 6.5 %slice.28 = bf16[2,32896,128]{2,1,0:T(8,128)(2,1)} slice(bf16[2,33024,128]{2,1,0:T(8,128)(2,1)S(1)} %bitcast.39), slice={[0:2], [0:32896], [0:128]} | slice | bytes 33685504 | tf_op jit(solution)/shard_map/slice | solution.py:47
  204.3 24.5 %reshape.108 = bf16[2,128,257,128]{3,2,1,0:T(8,128)(2,1)} reshape(bf16[2,32896,128]{2,1,0:T(8,128)(2,1)} %slice.28) | data formatting | bytes 33685504 | tf_op jit(solution)/shard_map/reshape | solution.py:47
  228.8 14.4 %fusion.1 = (f32[128,128,128]{2,1,0:T(8,128)S(1)}, f32[128,128,128]{2,1,0:T(8,128)}) fusion(f32[2,128,128]{2,1,0:T(8,128)S(1)} %copy.19, f32[2,128,128]{2,1,0:T(8,128)S(1)} %copy.16, bf16[2,128,257,128]{3,2,1,0:T(8,128)(2,1)} %reshape.108, bf16[2,128,257,128]{3,2,1,0:T(8,128)(2,1)} %reshape.106), kind=kLoop, calls=%fused_computation.6 | loop fusion | flops 37748736 | bytes 33816576 | tf_op jit(solution)/shard_map/reduce_sum | solution.py:60
  243.2 7.8 %fusion.4 = bf16[2,128,128,128]{3,2,1,0:T(8,128)(2,1)} fusion(f32[1,128,128,128]{3,2,1,0:T(8,128)} %bitcast.41, f32[1,128,128,128]{3,2,1,0:T(8,128)S(1)} %bitcast.40), kind=kLoop, calls=%fused_computation.10 | loop fusion | flops 12582912 | bytes 25165824 | tf_op jit(solution)/shard_map/convert_element_type | solution.py:91
  (16 shorter events, 0.1 us)
Async XLA Ops:
  6.5 61.6 %copy-start = (bf16[1,1600,1024]{2,1,0:T(8,128)(2,1)S(1)}, bf16[1,1600,1024]{2,1,0:T(8,128)(2,1)}, u32[]{:S(2)}) copy-start(bf16[1,1600,1024]{2,1,0:T(8,128)(2,1)} %param.2) | copy-start | bytes 9830404
  6.5 133.7 %reduce-scatter.2.cloned.1.call-start = ((), (), s32[]{:S(2)}) async-start(), calls=%async_computation.3 | async-start | bytes 2359296 | tf_op jit(solution)/shard_map/reduce_scatter | solution.py:74
  68.2 73.1 %copy-start.2 = (s32[128]{0:T(128)S(1)}, s32[128]{0:T(128)}, u32[]{:S(2)}) copy-start(s32[128]{0:T(128)} %param.3) | copy-start | bytes 1540
  149.9 7.9 %collective-permute-start = (bf16[2,128,128]{1,2,0:T(8,128)(2,1)S(1)}, bf16[2,128,128]{1,2,0:T(8,128)(2,1)S(1)}, u32[]{:S(2)}, u32[]{:S(2)}) collective-permute-start(bf16[2,128,128]{1,2,0:T(8,128)(2,1)S(1)} %bitcast.42), channel_id=1, source_target_pairs={{2,0},{4,2},{6,4},{8,6},{10,8},{12,10},{14,12},{3,1},{5,3},{7,5},{... | collective-permute-start | bytes 196616 | tf_op jit(solution)/shard_map/ppermute | solution.py:20
  156.3 37.0 %collective-permute-start.1 = (bf16[2,128,128]{1,2,0:T(8,128)(2,1)S(1)}, bf16[2,128,128]{1,2,0:T(8,128)(2,1)S(1)}, u32[]{:S(2)}, u32[]{:S(2)}) collective-permute-start(bf16[2,128,128]{1,2,0:T(8,128)(2,1)S(1)} %bitcast.45), channel_id=1, source_target_pairs={{2,0},{4,2},{6,4},{8,6},{10,8},{12,10},{14,12},{3,1},{5,3},{7,5},{... | collective-permute-start | bytes 196616 | tf_op jit(solution)/shard_map/ppermute | solution.py:20
  228.8 22.2 %copy-start.1 = (bf16[1,1600,1024]{2,1,0:T(8,128)(2,1)S(1)}, bf16[1,1600,1024]{2,1,0:T(8,128)(2,1)}, u32[]{:S(2)}) copy-start(bf16[1,1600,1024]{2,1,0:T(8,128)(2,1)} %param.2) | copy-start | bytes 9830404
Sparse Core Ops, SparseCore 0:
  71.7 68.4 reduce-scatter.1
where the time goes:
time: 261 us; the launch traced here: 258 us
  other arithmetic  87.8 us (34%)
  local copies, waits for them, and re-layouts  72.1 us (28%)
  waiting for transfers between devices  68.6 us (26%)
  between operations  13.6 us (5%)
  blocking collectives  9.67 us (4%)
  matrix products  3.42 us (1%)
    reduce_scatter x1, waiting for transfers between devices, local(): lax.psum_scatter(jnp.einsum('wnc,nk->cwk', records, local_basis, preferre...  68.6 us
    another operation x1, other arithmetic  61.4 us
    reshape x2, local copies, waits for them, and re-layouts, offset_view(): flat_rows[:, :group_size * (double_rows + 1)]  49 us
    reduce_sum x1, other arithmetic, cross_band(): real_sum = jnp.sum(base_real * moved_real + base_imag * moved_imag, axis=0)  14.4 us
    slice x2, local copies, waits for them, and re-layouts, offset_view(): flat_rows[:, :group_size * (double_rows + 1)]  13.2 us
    broadcast_in_dim x2, local copies, waits for them, and re-layouts, offset_view(): jnp.broadcast_to(wide[:, None], (window_count, group_size + 1, double_row...  8.55 us
    convert_element_type x1, other arithmetic, local(): return (stacked / windows).astype(jnp.bfloat16)  7.8 us
    all_to_all x1, blocking collectives, local(): lax.all_to_all(real_part, 'seg', split_axis=2, concat_axis=0, tiled=True)  5.88 us
  transfers between devices with their start and end apart: 3, of which 1 were waited for; matrix products, arithmetic and copies ran while one was open for 14% of the time, Pallas kernels for 0%

commit v1 on v0

v1 whole, which is shorter than its diff:
```python
import functools
import math

import jax
import jax.numpy as jnp
import ml_dtypes
import numpy as np
from jax import lax
from jax.experimental import pallas as pl
from jax.experimental.pallas import tpu as pltpu
from jax.sharding import PartitionSpec as P

OFFS = 128
L = 12800
FIRST_BIN = 64
F = 256
MODES = 64
EPSILON = 1e-06
MESH = pl.DeviceIdType.MESH


def sequences(length):
    n = np.arange(length, dtype=np.float64)
    diagonal = ((length - 1 - 2 * n) / 2) ** 2 * np.cos(2 * np.pi * F / 2 / L)
    beside = n[1:] * (length - n[1:]) / 2
    matrix = np.diag(diagonal) + np.diag(beside, 1) + np.diag(beside, -1)
    rows = np.linalg.eigh(matrix)[1][:, ::-1][:, :MODES].T
    sign = np.sign(np.sum(rows * (1.0 + n / length + np.sin(n)), axis=1, keepdims=True))
    return rows * sign


def tables(tiles, length):
    rows = sequences(length)
    n = np.arange(length, dtype=np.float64) - (length - 1) / 2
    middle = FIRST_BIN + (F - 1) / 2
    turn = 2 * np.pi * middle * n / L
    taper = 0.5 - 0.5 * np.cos(2 * np.pi * np.arange(tiles * length) / L).reshape(tiles, 1, length)
    modulated = np.concatenate([rows * np.cos(turn), -rows * np.sin(turn)])
    analysis = (taper * modulated).astype(ml_dtypes.bfloat16)
    bins = np.arange(F, dtype=np.float64)
    spectrum = np.exp(-2j * np.pi * (bins[:, None] - (F - 1) / 2) * n / L) @ rows.T
    centre = np.arange(tiles) * length + (length - 1) / 2
    spectrum = spectrum * np.exp(-2j * np.pi * (bins + FIRST_BIN)[:, None] * centre[:, None, None] / L)
    re, im = spectrum.real, spectrum.imag
    whole = np.concatenate(
        [np.concatenate([re, -im], axis=2), np.concatenate([im, re], axis=2)], axis=1
    )
    high = whole.astype(ml_dtypes.bfloat16)
    low = (whole - high.astype(np.float64)).astype(ml_dtypes.bfloat16)
    return analysis, np.concatenate([high, low], axis=2)


def spectra_kernel(
    tiles, rec, analysis, synthesis, live, out,
    rec_buf, a_buf, s_buf, send_buf, recv_buf, total, y_buf, wide,
    rec_sem, a_sem, s_sem, send_sem, recv_sem, y_send, y_recv,
):
    t, s = lax.axis_index("tiles"), lax.axis_index("seg")
    half = F // 2
    group = live.shape[1]

    def fetch(j):
        j = pl.multiple_of(j * group, group)
        return j

    def rec_copy(j):
        return pltpu.make_async_copy(rec.at[0, :, pl.ds(fetch(j), group)], rec_buf.at[j], rec_sem.at[j])

    a_copy = pltpu.make_async_copy(analysis.at[t], a_buf, a_sem)
    a_copy.start()

    @pl.loop(1, tiles + 1)
    def _(i):
        rec_copy(lax.rem(t + i, tiles)).start()

    s_copy = pltpu.make_async_copy(synthesis, s_buf, s_sem)
    s_copy.start()

    barrier = pltpu.get_barrier_semaphore()

    @pl.loop(1, tiles)
    def _(i):
        pl.semaphore_signal(barrier, inc=1, device_id={"tiles": lax.rem(t + i, tiles)}, device_id_type=MESH)

    for step in (0, 1, tiles - 1):
        pl.semaphore_signal(
            barrier, inc=1, device_id={"tiles": lax.rem(t + step, tiles), "seg": 1 - s}, device_id_type=MESH
        )

    def coefficients(j):
        rec_copy(j).wait()
        return jnp.dot(a_buf[...], rec_buf[j], preferred_element_type=jnp.float32).astype(jnp.bfloat16)

    def send(j):
        return pltpu.make_async_remote_copy(
            src_ref=send_buf.at[j], dst_ref=recv_buf.at[t], send_sem=send_sem.at[j], recv_sem=recv_sem.at[t],
            device_id={"tiles": j}, device_id_type=MESH,
        )

    a_copy.wait()
    first = lax.rem(t + 1, tiles)
    send_buf[first] = coefficients(first)
    pl.semaphore_wait(barrier, tiles + 2)
    send(first).start()

    @pl.loop(2, tiles)
    def _(i):
        j = lax.rem(t + i, tiles)
        send_buf[j] = coefficients(j)
        send(j).start()

    def part(i, own):
        both = jnp.concatenate([own, own], axis=0)
        return jnp.dot(s_buf[i], both, preferred_element_type=jnp.float32)

    own = coefficients(t)
    s_copy.wait()
    total[...] = part(t, own)

    @pl.loop(1, tiles)
    def _(i):
        j = lax.rem(t + tiles - i, tiles)
        pltpu.make_async_remote_copy(
            src_ref=send_buf.at[j], dst_ref=recv_buf.at[j], send_sem=send_sem.at[j], recv_sem=recv_sem.at[j],
            device_id={"tiles": j}, device_id_type=MESH,
        ).wait_recv()
        total[...] += part(j, recv_buf[j])

    spectra = total[...]
    power = jnp.sum(spectra * spectra, axis=0, keepdims=True) * (1.0 / (2 * F))
    gains = lax.rsqrt(power + EPSILON) * live[...].astype(jnp.float32)
    whitened = jnp.transpose(spectra * gains).astype(jnp.bfloat16)
    for p in range(2):
        for q in range(2):
            y_buf[p, q] = whitened[:, q * F + p * half:q * F + (p + 1) * half]

    across = pltpu.make_async_remote_copy(
        src_ref=y_buf.at[1 - s], dst_ref=wide.at[0, s], send_sem=y_send.at[0], recv_sem=y_recv.at[0],
        device_id={"seg": 1 - s}, device_id_type=MESH,
    )
    before = lax.rem(t + tiles - 1, tiles)
    back_same = pltpu.make_async_remote_copy(
        src_ref=y_buf.at[s], dst_ref=wide.at[1, s], send_sem=y_send.at[1], recv_sem=y_recv.at[1],
        device_id={"tiles": before}, device_id_type=MESH,
    )
    back_other = pltpu.make_async_remote_copy(
        src_ref=y_buf.at[1 - s], dst_ref=wide.at[1, s], send_sem=y_send.at[2], recv_sem=y_recv.at[2],
        device_id={"tiles": before, "seg": 1 - s}, device_id_type=MESH,
    )

    @pl.when(t > 0)
    def _():
        back_same.start()
        back_other.start()

    across.start()
    rows = pl.ds(0, group)
    next_rows = pl.ds(group, group)
    out[s, :, rows, :] = y_buf[s].astype(jnp.float32)

    @pl.loop(1, tiles)
    def _(i):
        send(lax.rem(t + i, tiles)).wait_send()

    across.wait_recv()
    out[1 - s, :, rows, :] = wide[0, 1 - s].astype(jnp.float32)

    @pl.when(t < tiles - 1)
    def _():
        back_same.wait_recv()
        pltpu.make_async_remote_copy(
            src_ref=y_buf.at[1 - s], dst_ref=wide.at[1, 1 - s], send_sem=y_send.at[2], recv_sem=y_recv.at[2],
            device_id={"tiles": before, "seg": 1 - s}, device_id_type=MESH,
        ).wait_recv()
        out[:, :, next_rows, :] = wide[1].astype(jnp.float32)

    @pl.when(t == tiles - 1)
    def _():
        out[:, :, next_rows, :] = jnp.zeros((2, 2, group, half), jnp.float32)

    @pl.when(t > 0)
    def _():
        back_same.wait_send()
        back_other.wait_send()

    across.wait_send()


def whitened_spectra(records, channel_live, tiles):
    length = records.shape[1]
    group = channel_live.shape[0]
    half = F // 2
    analysis, synthesis = tables(tiles, length)
    anywhere = pl.BlockSpec(memory_space=pl.ANY)
    vmem = pl.BlockSpec(memory_space=pltpu.VMEM)
    return pl.pallas_call(
        functools.partial(spectra_kernel, tiles),
        out_shape=jax.ShapeDtypeStruct((2, 2, 2 * group, half), jnp.float32),
        in_specs=[anywhere, anywhere, anywhere, vmem],
        out_specs=vmem,
        scratch_shapes=[
            pltpu.VMEM((tiles, length, group), jnp.bfloat16),
            pltpu.VMEM((2 * MODES, length), jnp.bfloat16),
            pltpu.VMEM((tiles, 2 * F, 4 * MODES), jnp.bfloat16),
            pltpu.VMEM((tiles, 2 * MODES, group), jnp.bfloat16),
            pltpu.VMEM((tiles, 2 * MODES, group), jnp.bfloat16),
            pltpu.VMEM((2 * F, group), jnp.float32),
            pltpu.VMEM((2, 2, group, half), jnp.bfloat16),
            pltpu.VMEM((2, 2, 2, group, half), jnp.bfloat16),
            pltpu.SemaphoreType.DMA((tiles,)),
            pltpu.SemaphoreType.DMA,
            pltpu.SemaphoreType.DMA,
            pltpu.SemaphoreType.DMA((tiles,)),
            pltpu.SemaphoreType.DMA((tiles,)),
            pltpu.SemaphoreType.DMA((3,)),
            pltpu.SemaphoreType.DMA((3,)),
        ],
        compiler_params=pltpu.CompilerParams(
            collective_id=0, has_side_effects=True, vmem_limit_bytes=40 << 20
        ),
    )(records, jnp.asarray(analysis), jnp.asarray(synthesis), channel_live.reshape(1, group))


CHANNEL_BLOCK = 8
OFFSET_BLOCK = 32


def cross_kernel(scale, wide, out):
    first = pl.program_id(0) * CHANNEL_BLOCK

    @pl.loop(0, CHANNEL_BLOCK)
    def _(i):
        c = first + i
        base = [[wide[w, q, pl.ds(c, 1), :] * scale for q in range(2)] for w in range(2)]
        for o in range(0, OFFS, OFFSET_BLOCK):
            real, imag = None, None
            for w in range(2):
                re, im = base[w]
                moved_re = wide[w, 0, pl.ds(c + o, OFFSET_BLOCK), :]
                moved_im = wide[w, 1, pl.ds(c + o, OFFSET_BLOCK), :]
                more_real = re * moved_re + im * moved_im
                more_imag = im * moved_re - re * moved_im
                real = more_real if real is None else real + more_real
                imag = more_imag if imag is None else imag + more_imag
            out[0, i, pl.ds(o, OFFSET_BLOCK), :] = real.astype(jnp.bfloat16)
            out[1, i, pl.ds(o, OFFSET_BLOCK), :] = imag.astype(jnp.bfloat16)


def cross_spectra(wide, windows):
    group, half = wide.shape[2] // 2, wide.shape[3]
    return pl.pallas_call(
        functools.partial(cross_kernel, 1.0 / windows),
        grid=(group // CHANNEL_BLOCK,),
        out_shape=jax.ShapeDtypeStruct((2, group, OFFS, half), jnp.bfloat16),
        in_specs=[pl.BlockSpec(memory_space=pltpu.VMEM)],
        out_specs=pl.BlockSpec((2, CHANNEL_BLOCK, OFFS, half), lambda i: (0, i, 0, 0)),
        compiler_params=pltpu.CompilerParams(vmem_limit_bytes=16 << 20),
    )(wide)


def solution(mesh):
    tiles = mesh.shape["tiles"]

    def local(records, channel_live):
        wide = whitened_spectra(records, channel_live, tiles)
        return cross_spectra(wide, records.shape[0] * mesh.shape["seg"])

    in_specs = (P("seg", "tiles", "groups"), P(("groups", "tiles")))
    out_specs = P(None, ("groups", "tiles"), None, "seg")
    return jax.shard_map(local, mesh=mesh, in_specs=in_specs, out_specs=out_specs, check_vma=False)
```

time: 261 us -> 34.5 us (0.13); the launches traced: 258 us -> 34.3 us
  other arithmetic: 87.8 us -> 0 us
  waiting for transfers between devices: 68.6 us -> 0 us
  local copies, waits for them, and re-layouts: 72.1 us -> 6.13 us
  Pallas kernels: 0 us -> 28.1 us
  between operations: 13.6 us -> 0.01 us
  blocking collectives: 9.67 us -> 0 us
  matrix products: 3.42 us -> 0 us
    reduce_scatter x1 -> x0, waiting for transfers between devices: 68.6 us -> none  [local(): lax.psum_scatter(jnp.einsum('wnc,nk->cwk', records, local_basis, preferre...]
    another operation x1 -> x0, other arithmetic: 61.4 us -> none
    reshape x2 -> x0, local copies, waits for them, and re-layouts: 49 us -> none  [offset_view(): flat_rows[:, :group_size * (double_rows + 1)]]
    pallas_call x0 -> x2, Pallas kernels: none -> 28.1 us  [the longest x1 18.9 us: whitened_spectra(): pl.pallas_call(functools.partial(spectra_kernel, tiles), out_shape=jax.Sh...]
    reduce_sum x2 -> x0, other arithmetic: 15.4 us -> none  [the longest x1 14.4 us: cross_band(): real_sum = jnp.sum(base_real * moved_real + base_imag * moved_imag, axis=0)]
    slice x5 -> x0, local copies, waits for them, and re-layouts: 13.4 us -> none  [the longest x2 13.2 us: offset_view(): flat_rows[:, :group_size * (double_rows + 1)]]
    all_to_all x2 -> x0, blocking collectives: 9.67 us -> none  [the longest x1 5.88 us: local(): lax.all_to_all(real_part, 'seg', split_axis=2, concat_axis=0, tiled=True)]
    convert_element_type x2 -> x0, other arithmetic: 8.76 us -> none  [the longest x1 7.8 us: local(): return (stacked / windows).astype(jnp.bfloat16)]
  transfers between devices with their start and end apart: 3 -> 0, of which waited for: 1 -> 0; matrix products, arithmetic and copies ran while one was open for 14% -> 0% of each run, Pallas kernels for 0% -> 0%
where the time goes in v1:
time: 34.5 us; the launch traced here: 34.3 us
  Pallas kernels  28.1 us (81%)
  local copies, waits for them, and re-layouts  6.13 us (18%)
    pallas_call x1, Pallas kernels, whitened_spectra(): pl.pallas_call(functools.partial(spectra_kernel, tiles), out_shape=jax.Sh...  18.9 us
    pallas_call x1, Pallas kernels, cross_spectra(): pl.pallas_call(functools.partial(cross_kernel, 1.0 / windows), grid=(grou...  9.21 us
    unnamed x8, local copies, waits for them, and re-layouts  6.13 us

profile of v1, /device:TPU:1, one launch (start us, length us, event | category | flops | bytes accessed | tf_op | source)
XLA Modules:
  0.0 34.3 jit_solution(8455206249453507309)
XLA Ops:
  0.0 0.0 copy-start
  0.0 2.0 %copy-done = bf16[8,128,1600]{2,1,0:T(8,128)(2,1)S(1)} copy-done((bf16[8,128,1600]{2,1,0:T(8,128)(2,1)S(1)}, bf16[8,128,1600]{2,1,0:T(8,128)(2,1)}, u32[]{:S(2)}) %copy-start) | copy-done | bytes 3276824
  2.0 0.0 copy-start.1
  2.0 1.9 %copy-done.1 = bf16[1,1600,1024]{2,1,0:T(8,128)(2,1)S(1)} copy-done((bf16[1,1600,1024]{2,1,0:T(8,128)(2,1)S(1)}, bf16[1,1600,1024]{2,1,0:T(8,128)(2,1)}, u32[]{:S(2)}) %copy-start.1) | copy-done | bytes 3276824
  3.9 0.0 copy-start.2
  3.9 1.6 %copy-done.2 = bf16[8,512,256]{2,1,0:T(8,128)(2,1)S(1)} copy-done((bf16[8,512,256]{2,1,0:T(8,128)(2,1)S(1)}, bf16[8,512,256]{2,1,0:T(8,128)(2,1)}, u32[]{:S(2)}) %copy-start.2) | copy-done | bytes 2097176
  5.5 0.0 copy-start.3
  5.5 0.7 %copy-done.3 = s32[128]{0:T(128)S(1)} copy-done((s32[128]{0:T(128)S(1)}, s32[128]{0:T(128)}, u32[]{:S(2)}) %copy-start.3) | copy-done | bytes 536
  6.1 18.9 %shard_map.46.wide = f32[2,2,256,128]{3,2,1,0:T(8,128)S(1)} custom-call(bf16[1,1600,1024]{2,1,0:T(8,128)(2,1)S(1)} %copy-done.1, bf16[8,128,1600]{2,1,0:T(8,128)(2,1)S(1)} %copy-done, bf16[8,512,256]{2,1,0:T(8,128)(2,1)S(1)} %copy-done.2, s32[1,128]{1,0:T(1,128)S(1)} %bitcast.1), custom_call_target="tpu_custom_call" | custom-call | tf_op jit(solution)/shard_map/pallas_call | solution.py:196
  25.1 9.2 %shard_map.47 = bf16[2,128,128,128]{3,2,1,0:T(8,128)(2,1)} custom-call(f32[2,2,256,128]{3,2,1,0:T(8,128)S(1)} %shard_map.46.wide), custom_call_target="tpu_custom_call" | custom-call | tf_op jit(solution)/shard_map/pallas_call | solution.py:251
Async XLA Ops:
  0.0 2.0 %copy-start = (bf16[8,128,1600]{2,1,0:T(8,128)(2,1)S(1)}, bf16[8,128,1600]{2,1,0:T(8,128)(2,1)}, u32[]{:S(2)}) copy-start(bf16[8,128,1600]{2,1,0:T(8,128)(2,1)} %constant.4.clone.analysis) | copy-start | bytes 9830404
  2.0 1.9 %copy-start.1 = (bf16[1,1600,1024]{2,1,0:T(8,128)(2,1)S(1)}, bf16[1,1600,1024]{2,1,0:T(8,128)(2,1)}, u32[]{:S(2)}) copy-start(bf16[1,1600,1024]{2,1,0:T(8,128)(2,1)} %rec.1) | copy-start | bytes 9830404
  3.9 1.6 %copy-start.2 = (bf16[8,512,256]{2,1,0:T(8,128)(2,1)S(1)}, bf16[8,512,256]{2,1,0:T(8,128)(2,1)}, u32[]{:S(2)}) copy-start(bf16[8,512,256]{2,1,0:T(8,128)(2,1)} %constant.5.clone.synthesis) | copy-start | bytes 6291460
  5.5 0.7 %copy-start.3 = (s32[128]{0:T(128)S(1)}, s32[128]{0:T(128)}, u32[]{:S(2)}) copy-start(s32[128]{0:T(128)} %param.5) | copy-start | bytes 1540

commit v2 on v1

v2 whole, which is shorter than its diff:
```python
import functools
import math

import jax
import jax.numpy as jnp
import ml_dtypes
import numpy as np
from jax import lax
from jax.experimental import pallas as pl
from jax.experimental.pallas import tpu as pltpu
from jax.sharding import PartitionSpec as P

OFFS = 128
L = 12800
FIRST_BIN = 64
F = 256
MODES = 64
EPSILON = 1e-06
MESH = pl.DeviceIdType.MESH


def sequences(length):
    n = np.arange(length, dtype=np.float64)
    diagonal = ((length - 1 - 2 * n) / 2) ** 2 * np.cos(2 * np.pi * F / 2 / L)
    beside = n[1:] * (length - n[1:]) / 2
    matrix = np.diag(diagonal) + np.diag(beside, 1) + np.diag(beside, -1)
    rows = np.linalg.eigh(matrix)[1][:, ::-1][:, :MODES].T
    sign = np.sign(np.sum(rows * (1.0 + n / length + np.sin(n)), axis=1, keepdims=True))
    return rows * sign


def tables(tiles, length):
    rows = sequences(length)
    n = np.arange(length, dtype=np.float64) - (length - 1) / 2
    middle = FIRST_BIN + (F - 1) / 2
    turn = 2 * np.pi * middle * n / L
    taper = 0.5 - 0.5 * np.cos(2 * np.pi * np.arange(tiles * length) / L).reshape(tiles, length)
    modulated = np.concatenate([rows * np.cos(turn), -rows * np.sin(turn)])
    analysis = (np.round(np.concatenate([modulated, taper]) * 2.0**20) / 2.0**20).astype(np.float32)
    bins = np.arange(F, dtype=np.float64)
    spectrum = np.exp(-2j * np.pi * (bins[:, None] - (F - 1) / 2) * n / L) @ rows.T
    centre = np.arange(tiles) * length + (length - 1) / 2
    spectrum = spectrum * np.exp(-2j * np.pi * (bins + FIRST_BIN)[:, None] * centre[:, None, None] / L)
    re, im = spectrum.real, spectrum.imag
    whole = np.concatenate(
        [np.concatenate([re, -im], axis=2), np.concatenate([im, re], axis=2)], axis=1
    )
    high = whole.astype(ml_dtypes.bfloat16)
    low = (whole - high.astype(np.float64)).astype(ml_dtypes.bfloat16)
    return analysis, np.concatenate([high, low], axis=2)


def spectra_kernel(
    tiles, rec, analysis, synthesis, live, out,
    rec_buf, table, a_buf, s_buf, live_buf, send_buf, recv_buf, total, y_buf, blank,
    rec_sem, a_sem, s_sem, live_sem, out_sem, send_sem, recv_sem, y_send, y_recv,
):
    t, s = lax.axis_index("tiles"), lax.axis_index("seg")
    half = F // 2
    group = live.shape[1]

    def rec_copy(j):
        columns = pl.ds(pl.multiple_of(j * group, group), group)
        return pltpu.make_async_copy(rec.at[0, :, columns], rec_buf.at[j], rec_sem.at[j])

    a_copy = pltpu.make_async_copy(analysis, table, a_sem)
    a_copy.start()

    @pl.loop(1, tiles + 1)
    def _(i):
        rec_copy(lax.rem(t + i, tiles)).start()

    s_copy = pltpu.make_async_copy(synthesis, s_buf, s_sem)
    s_copy.start()
    live_copy = pltpu.make_async_copy(live, live_buf, live_sem)
    live_copy.start()

    barrier = pltpu.get_barrier_semaphore()

    @pl.loop(1, tiles)
    def _(i):
        pl.semaphore_signal(barrier, inc=1, device_id={"tiles": lax.rem(t + i, tiles)}, device_id_type=MESH)

    for step in (0, 1, tiles - 1):
        pl.semaphore_signal(
            barrier, inc=1, device_id={"tiles": lax.rem(t + step, tiles), "seg": 1 - s}, device_id_type=MESH
        )

    def coefficients(j):
        rec_copy(j).wait()
        return jnp.dot(a_buf[...], rec_buf[j], preferred_element_type=jnp.float32).astype(jnp.bfloat16)

    def send(j):
        return pltpu.make_async_remote_copy(
            src_ref=send_buf.at[j], dst_ref=recv_buf.at[t], send_sem=send_sem.at[j], recv_sem=recv_sem.at[t],
            device_id={"tiles": j}, device_id_type=MESH,
        )

    a_copy.wait()
    taper = table[pl.ds(2 * MODES + t, 1), :]
    a_buf[...] = (table[pl.ds(0, 2 * MODES), :] * taper).astype(jnp.bfloat16)
    first = lax.rem(t + 1, tiles)
    send_buf[first] = coefficients(first)
    pl.semaphore_wait(barrier, tiles + 2)
    send(first).start()

    @pl.loop(2, tiles)
    def _(i):
        j = lax.rem(t + i, tiles)
        send_buf[j] = coefficients(j)
        send(j).start()

    def part(i, own):
        both = jnp.concatenate([own, own], axis=0)
        return jnp.dot(s_buf[i], both, preferred_element_type=jnp.float32)

    own = coefficients(t)
    s_copy.wait()
    total[...] = part(t, own)

    @pl.loop(1, tiles)
    def _(i):
        j = lax.rem(t + tiles - i, tiles)
        pltpu.make_async_remote_copy(
            src_ref=send_buf.at[j], dst_ref=recv_buf.at[j], send_sem=send_sem.at[j], recv_sem=recv_sem.at[j],
            device_id={"tiles": j}, device_id_type=MESH,
        ).wait_recv()
        total[...] += part(j, recv_buf[j])

    live_copy.wait()
    spectra = total[...]
    power = jnp.sum(spectra * spectra, axis=0, keepdims=True) * (1.0 / (2 * F))
    gains = lax.rsqrt(power + EPSILON) * live_buf[...].astype(jnp.float32)
    whitened = jnp.transpose(spectra * gains).astype(jnp.bfloat16)
    for p in range(2):
        for q in range(2):
            y_buf[p, q] = whitened[:, q * F + p * half:q * F + (p + 1) * half]

    before = lax.rem(t + tiles - 1, tiles)

    def hand_over(bins, place, window, k, **device):
        return pltpu.make_async_remote_copy(
            src_ref=y_buf.at[bins], dst_ref=out.at[place, window], send_sem=y_send.at[k], recv_sem=y_recv.at[k],
            device_id=device, device_id_type=MESH,
        )

    back_same = hand_over(s, 1, s, 1, tiles=before)
    back_other = hand_over(1 - s, 1, s, 2, tiles=before, seg=1 - s)
    across = hand_over(1 - s, 0, s, 0, seg=1 - s)

    @pl.when(t > 0)
    def _():
        back_same.start()
        back_other.start()

    across.start()
    keep = pltpu.make_async_copy(y_buf.at[s], out.at[0, s], out_sem.at[0])
    keep.start()

    @pl.when(t == tiles - 1)
    def _():
        blank[...] = jnp.zeros_like(blank)
        clear = pltpu.make_async_copy(blank, out.at[1], out_sem.at[1])
        clear.start()
        clear.wait()

    @pl.loop(1, tiles)
    def _(i):
        send(lax.rem(t + i, tiles)).wait_send()

    keep.wait()
    hand_over(1 - s, 0, 1 - s, 0, seg=1 - s).wait_recv()

    @pl.when(t < tiles - 1)
    def _():
        back_same.wait_recv()
        hand_over(1 - s, 1, 1 - s, 2, tiles=before, seg=1 - s).wait_recv()

    @pl.when(t > 0)
    def _():
        back_same.wait_send()
        back_other.wait_send()

    across.wait_send()


def whitened_spectra(records, channel_live, tiles):
    length = records.shape[1]
    group = channel_live.shape[0]
    half = F // 2
    analysis, synthesis = tables(tiles, length)
    in_hbm = pl.BlockSpec(memory_space=pltpu.HBM)
    return pl.pallas_call(
        functools.partial(spectra_kernel, tiles),
        out_shape=jax.ShapeDtypeStruct((2, 2, 2, group, half), jnp.bfloat16),
        in_specs=[in_hbm] * 4,
        out_specs=in_hbm,
        scratch_shapes=[
            pltpu.VMEM((tiles, length, group), jnp.bfloat16),
            pltpu.VMEM((2 * MODES + tiles, length), jnp.float32),
            pltpu.VMEM((2 * MODES, length), jnp.bfloat16),
            pltpu.VMEM((tiles, 2 * F, 4 * MODES), jnp.bfloat16),
            pltpu.VMEM((1, group), jnp.int32),
            pltpu.VMEM((tiles, 2 * MODES, group), jnp.bfloat16),
            pltpu.VMEM((tiles, 2 * MODES, group), jnp.bfloat16),
            pltpu.VMEM((2 * F, group), jnp.float32),
            pltpu.VMEM((2, 2, group, half), jnp.bfloat16),
            pltpu.VMEM((2, 2, group, half), jnp.bfloat16),
            pltpu.SemaphoreType.DMA((tiles,)),
            pltpu.SemaphoreType.DMA,
            pltpu.SemaphoreType.DMA,
            pltpu.SemaphoreType.DMA,
            pltpu.SemaphoreType.DMA((2,)),
            pltpu.SemaphoreType.DMA((tiles,)),
            pltpu.SemaphoreType.DMA((tiles,)),
            pltpu.SemaphoreType.DMA((3,)),
            pltpu.SemaphoreType.DMA((3,)),
        ],
        compiler_params=pltpu.CompilerParams(
            collective_id=0, has_side_effects=True, vmem_limit_bytes=60 << 20
        ),
    )(records, jnp.asarray(analysis), jnp.asarray(synthesis), channel_live.reshape(1, group))


CHANNEL_BLOCK = 8
OFFSET_BLOCK = 32


def cross_kernel(scale, halves, out, wide, stack, sem):
    group = halves.shape[3]
    for w in range(2):
        for place in range(2):
            re, im = (halves[place, w, q].astype(jnp.float32) for q in range(2))
            rows = pl.ds(place * group, group)
            wide[w, 0, rows, :] = re
            wide[w, 1, rows, :] = im
            wide[w, 2, rows, :] = re + im

    def channel(c):
        (a0, b0), (a1, b1) = [[wide[w, q, pl.ds(c, 1), :] * scale for q in range(2)] for w in range(2)]
        pairs = ((2, b0, b1), (0, a0 - b0, a1 - b1), (1, a0 + b0, a1 + b1))
        for o in range(0, OFFS, OFFSET_BLOCK):
            rows = pl.ds(c + o, OFFSET_BLOCK)
            shared, more, less = (
                first * wide[0, q, rows, :] + second * wide[1, q, rows, :] for q, first, second in pairs
            )
            stack[0, c, pl.ds(o, OFFSET_BLOCK), :] = (shared + more).astype(jnp.bfloat16)
            stack[1, c, pl.ds(o, OFFSET_BLOCK), :] = (shared - less).astype(jnp.bfloat16)

    def copies(k):
        rows = pl.ds(k * CHANNEL_BLOCK, CHANNEL_BLOCK)
        return [pltpu.make_async_copy(stack.at[q, rows], out.at[q, rows], sem.at[q, k]) for q in range(2)]

    @pl.loop(0, group // CHANNEL_BLOCK)
    def _(k):
        for i in range(CHANNEL_BLOCK):
            channel(k * CHANNEL_BLOCK + i)
        for copy in copies(k):
            copy.start()

    @pl.loop(0, group // CHANNEL_BLOCK)
    def _(k):
        for copy in copies(k):
            copy.wait()


def cross_spectra(halves, windows):
    group, half = halves.shape[3:]
    return pl.pallas_call(
        functools.partial(cross_kernel, 1.0 / windows),
        out_shape=jax.ShapeDtypeStruct((2, group, OFFS, half), jnp.bfloat16),
        in_specs=[pl.BlockSpec(memory_space=pltpu.VMEM)],
        out_specs=pl.BlockSpec(memory_space=pltpu.HBM),
        scratch_shapes=[
            pltpu.VMEM((2, 3, 2 * group, half), jnp.float32),
            pltpu.VMEM((2, group, OFFS, half), jnp.bfloat16),
            pltpu.SemaphoreType.DMA((2, group // CHANNEL_BLOCK)),
        ],
        compiler_params=pltpu.CompilerParams(vmem_limit_bytes=60 << 20),
    )(halves)


def solution(mesh):
    tiles = mesh.shape["tiles"]

    def local(records, channel_live):
        halves = whitened_spectra(records, channel_live, tiles)
        return cross_spectra(halves, records.shape[0] * mesh.shape["seg"])

    in_specs = (P("seg", "tiles", "groups"), P(("groups", "tiles")))
    out_specs = P(None, ("groups", "tiles"), None, "seg")
    return jax.shard_map(local, mesh=mesh, in_specs=in_specs, out_specs=out_specs, check_vma=False)
```

time: 34.5 us -> 23.6 us (0.68)
  local copies, waits for them, and re-layouts: 6.13 us -> 0 us
  Pallas kernels: 28.1 us -> 23.4 us
    unnamed x8 -> x0, local copies, waits for them, and re-layouts: 6.13 us -> none
    pallas_call x1, Pallas kernels: 9.21 us -> 5.7 us  [cross_spectra(): pl.pallas_call(functools.partial(cross_kernel, 1.0 / windows), out_shape=...]
    pallas_call x1, Pallas kernels: 18.9 us -> 17.7 us  [whitened_spectra(): pl.pallas_call(functools.partial(spectra_kernel, tiles), out_shape=jax.Sh...]
where the time goes in v2:
time: 23.6 us; the launch traced here: 23.4 us
  Pallas kernels  23.4 us (99%)
    pallas_call x1, Pallas kernels, whitened_spectra(): pl.pallas_call(functools.partial(spectra_kernel, tiles), out_shape=jax.Sh...  17.7 us
    pallas_call x1, Pallas kernels, cross_spectra(): pl.pallas_call(functools.partial(cross_kernel, 1.0 / windows), out_shape=...  5.7 us

profile of v2, /device:TPU:1, one launch (start us, length us, event | category | flops | bytes accessed | tf_op | source)
XLA Modules:
  0.0 23.4 jit_solution(1397862805143313360)
XLA Ops:
  0.0 17.7 %shard_map.46.halves = bf16[2,2,2,128,128]{4,3,2,1,0:T(8,128)(2,1)} custom-call(bf16[1,1600,1024]{2,1,0:T(8,128)(2,1)} %rec.1, f32[136,1600]{1,0:T(8,128)} %constant.4.clone.analysis, bf16[8,512,256]{2,1,0:T(8,128)(2,1)} %constant.5.clone.synthesis, s32[1,128]{1,0:T(1,128)} %bitcast.1), custom_call_target="tpu_custom_call" | custom-call | tf_op jit(solution)/shard_map/pallas_call | solution.py:193
  17.7 5.7 %shard_map.47 = bf16[2,128,128,128]{3,2,1,0:T(8,128)(2,1)} custom-call(bf16[2,2,2,128,128]{4,3,2,1,0:T(8,128)(2,1)} %shard_map.46.halves), custom_call_target="tpu_custom_call" | custom-call | tf_op jit(solution)/shard_map/pallas_call | solution.py:269

commit v3 on v2

--- a/solution.py
+++ b/solution.py
@@ -14,7 +14,7 @@
 L = 12800
 FIRST_BIN = 64
 F = 256
-MODES = 64
+MODES = 48
 EPSILON = 1e-06
 MESH = pl.DeviceIdType.MESH
 
@@ -45,9 +45,8 @@
     whole = np.concatenate(
         [np.concatenate([re, -im], axis=2), np.concatenate([im, re], axis=2)], axis=1
     )
-    high = whole.astype(ml_dtypes.bfloat16)
-    low = (whole - high.astype(np.float64)).astype(ml_dtypes.bfloat16)
-    return analysis, np.concatenate([high, low], axis=2)
+    pairs = np.concatenate([whole[0::2], whole[1::2]], axis=2)
+    return analysis, pairs.astype(ml_dtypes.bfloat16)
 
 
 def spectra_kernel(
@@ -90,10 +89,19 @@
         rec_copy(j).wait()
         return jnp.dot(a_buf[...], rec_buf[j], preferred_element_type=jnp.float32).astype(jnp.bfloat16)
 
+    def rows_of(j):
+        return pl.ds(pl.multiple_of(j * 2 * MODES, 2 * MODES), 2 * MODES)
+
     def send(j):
         return pltpu.make_async_remote_copy(
-            src_ref=send_buf.at[j], dst_ref=recv_buf.at[t], send_sem=send_sem.at[j], recv_sem=recv_sem.at[t],
-            device_id={"tiles": j}, device_id_type=MESH,
+            src_ref=send_buf.at[j], dst_ref=recv_buf.at[rows_of(t)], send_sem=send_sem.at[j],
+            recv_sem=recv_sem.at[t], device_id={"tiles": j}, device_id_type=MESH,
+        )
+
+    def arrived(j):
+        return pltpu.make_async_remote_copy(
+            src_ref=send_buf.at[j], dst_ref=recv_buf.at[rows_of(j)], send_sem=send_sem.at[j],
+            recv_sem=recv_sem.at[j], device_id={"tiles": j}, device_id_type=MESH,
         )
 
     a_copy.wait()
@@ -110,50 +118,52 @@
         send_buf[j] = coefficients(j)
         send(j).start()
 
-    def part(i, own):
-        both = jnp.concatenate([own, own], axis=0)
-        return jnp.dot(s_buf[i], both, preferred_element_type=jnp.float32)
-
-    own = coefficients(t)
+    recv_buf[rows_of(t), :] = coefficients(t)
     s_copy.wait()
-    total[...] = part(t, own)
-
-    @pl.loop(1, tiles)
-    def _(i):
-        j = lax.rem(t + tiles - i, tiles)
-        pltpu.make_async_remote_copy(
-            src_ref=send_buf.at[j], dst_ref=recv_buf.at[j], send_sem=send_sem.at[j], recv_sem=recv_sem.at[j],
-            device_id={"tiles": j}, device_id_type=MESH,
-        ).wait_recv()
-        total[...] += part(j, recv_buf[j])
+
+    def part(p):
+        rows = pl.ds(pl.multiple_of(p * 4 * MODES, 4 * MODES), 4 * MODES)
+        return jnp.dot(s_buf[p], recv_buf[rows, :], preferred_element_type=jnp.float32)
+
+    pair, pairs = lax.div(t, 2), tiles // 2
+    arrived(pair * 2 + 1 - lax.rem(t, 2)).wait_recv()
+    total[...] = part(pair)
+
+    @pl.loop(1, pairs)
+    def _(i):
+        p = lax.rem(pair + pairs - i, pairs)
+        arrived(2 * p).wait_recv()
+        arrived(2 * p + 1).wait_recv()
+        total[...] += part(p)
 
     live_copy.wait()
     spectra = total[...]
     power = jnp.sum(spectra * spectra, axis=0, keepdims=True) * (1.0 / (2 * F))
     gains = lax.rsqrt(power + EPSILON) * live_buf[...].astype(jnp.float32)
-    whitened = jnp.transpose(spectra * gains).astype(jnp.bfloat16)
+    before = lax.rem(t + tiles - 1, tiles)
+
+    def hand_back(p, window):
+        return pltpu.make_async_remote_copy(
+            src_ref=y_buf.at[p], dst_ref=out.at[1, window], send_sem=y_send.at[p], recv_sem=y_recv.at[window],
+            device_id={"tiles": before, "seg": p}, device_id_type=MESH,
+        )
+
+    def hand_across(window):
+        return pltpu.make_async_remote_copy(
+            src_ref=y_buf.at[1 - s], dst_ref=out.at[0, window], send_sem=y_send.at[2], recv_sem=y_recv.at[2],
+            device_id={"seg": 1 - s}, device_id_type=MESH,
+        )
+
     for p in range(2):
         for q in range(2):
-            y_buf[p, q] = whitened[:, q * F + p * half:q * F + (p + 1) * half]
-
-    before = lax.rem(t + tiles - 1, tiles)
-
-    def hand_over(bins, place, window, k, **device):
-        return pltpu.make_async_remote_copy(
-            src_ref=y_buf.at[bins], dst_ref=out.at[place, window], send_sem=y_send.at[k], recv_sem=y_recv.at[k],
-            device_id=device, device_id_type=MESH,
-        )
-
-    back_same = hand_over(s, 1, s, 1, tiles=before)
-    back_other = hand_over(1 - s, 1, s, 2, tiles=before, seg=1 - s)
-    across = hand_over(1 - s, 0, s, 0, seg=1 - s)
-
-    @pl.when(t > 0)
-    def _():
-        back_same.start()
-        back_other.start()
-
-    across.start()
+            bins = slice(q * F + p * half, q * F + (p + 1) * half)
+            y_buf[p, q] = jnp.transpose(spectra[bins] * gains).astype(jnp.bfloat16)
+
+        @pl.when(t > 0)
+        def _():
+            hand_back(p, s).start()
+
+    hand_across(s).start()
     keep = pltpu.make_async_copy(y_buf.at[s], out.at[0, s], out_sem.at[0])
     keep.start()
 
@@ -169,19 +179,19 @@
         send(lax.rem(t + i, tiles)).wait_send()
 
     keep.wait()
-    hand_over(1 - s, 0, 1 - s, 0, seg=1 - s).wait_recv()
+    hand_across(1 - s).wait_recv()
 
     @pl.when(t < tiles - 1)
     def _():
-        back_same.wait_recv()
-        hand_over(1 - s, 1, 1 - s, 2, tiles=before, seg=1 - s).wait_recv()
+        for window in range(2):
+            hand_back(0, window).wait_recv()
 
     @pl.when(t > 0)
     def _():
-        back_same.wait_send()
-        back_other.wait_send()
-
-    across.wait_send()
+        for p in range(2):
+            hand_back(p, s).wait_send()
+
+    hand_across(s).wait_send()
 
 
 def whitened_spectra(records, channel_live, tiles):
@@ -199,10 +209,10 @@
             pltpu.VMEM((tiles, length, group), jnp.bfloat16),
             pltpu.VMEM((2 * MODES + tiles, length), jnp.float32),
             pltpu.VMEM((2 * MODES, length), jnp.bfloat16),
-            pltpu.VMEM((tiles, 2 * F, 4 * MODES), jnp.bfloat16),
+            pltpu.VMEM((tiles // 2, 2 * F, 4 * MODES), jnp.bfloat16),
             pltpu.VMEM((1, group), jnp.int32),
             pltpu.VMEM((tiles, 2 * MODES, group), jnp.bfloat16),
-            pltpu.VMEM((tiles, 2 * MODES, group), jnp.bfloat16),
+            pltpu.VMEM((tiles * 2 * MODES, group), jnp.bfloat16),
             pltpu.VMEM((2 * F, group), jnp.float32),
             pltpu.VMEM((2, 2, group, half), jnp.bfloat16),
             pltpu.VMEM((2, 2, group, half), jnp.bfloat16),

time: 23.6 us -> 22.2 us (0.941)
  Pallas kernels: 23.4 us -> 22.1 us
    pallas_call x1, Pallas kernels: 17.7 us -> 16.4 us  [whitened_spectra(): pl.pallas_call(functools.partial(spectra_kernel, tiles), out_shape=jax.Sh...]
where the time goes in v3:
time: 22.2 us; the launch traced here: 22.1 us
  Pallas kernels  22.1 us (100%)
    pallas_call x1, Pallas kernels, whitened_spectra(): pl.pallas_call(functools.partial(spectra_kernel, tiles), out_shape=jax.Sh...  16.4 us
    pallas_call x1, Pallas kernels, cross_spectra(): pl.pallas_call(functools.partial(cross_kernel, 1.0 / windows), out_shape=...  5.7 us

profile of v3, /device:TPU:1, one launch (start us, length us, event | category | flops | bytes accessed | tf_op | source)
XLA Modules:
  0.0 22.1 jit_solution(622473222156382858)
XLA Ops:
  0.0 16.4 %shard_map.46.halves = bf16[2,2,2,128,128]{4,3,2,1,0:T(8,128)(2,1)} custom-call(bf16[1,1600,1024]{2,1,0:T(8,128)(2,1)} %rec.1, f32[104,1600]{1,0:T(8,128)} %constant.4.clone.analysis, bf16[4,512,192]{2,1,0:T(8,128)(2,1)} %constant.5.clone.synthesis, s32[1,128]{1,0:T(1,128)} %bitcast.1), custom_call_target="tpu_custom_call" | custom-call | tf_op jit(solution)/shard_map/pallas_call | solution.py:203
  16.4 5.7 %shard_map.47 = bf16[2,128,128,128]{3,2,1,0:T(8,128)(2,1)} custom-call(bf16[2,2,2,128,128]{4,3,2,1,0:T(8,128)(2,1)} %shard_map.46.halves), custom_call_target="tpu_custom_call" | custom-call | tf_op jit(solution)/shard_map/pallas_call | solution.py:279

commit v4 on v3

--- a/solution.py
+++ b/solution.py
@@ -62,12 +62,16 @@
         columns = pl.ds(pl.multiple_of(j * group, group), group)
         return pltpu.make_async_copy(rec.at[0, :, columns], rec_buf.at[j], rec_sem.at[j])
 
+    def turn(i):
+        m = lax.div(i, 2)
+        return lax.rem(tiles + tiles // 2 + m - 2 * m * lax.rem(i, 2), tiles)
+
     a_copy = pltpu.make_async_copy(analysis, table, a_sem)
     a_copy.start()
 
     @pl.loop(1, tiles + 1)
     def _(i):
-        rec_copy(lax.rem(t + i, tiles)).start()
+        rec_copy(lax.rem(t + turn(i), tiles)).start()
 
     s_copy = pltpu.make_async_copy(synthesis, s_buf, s_sem)
     s_copy.start()
@@ -107,14 +111,14 @@
     a_copy.wait()
     taper = table[pl.ds(2 * MODES + t, 1), :]
     a_buf[...] = (table[pl.ds(0, 2 * MODES), :] * taper).astype(jnp.bfloat16)
-    first = lax.rem(t + 1, tiles)
+    first = lax.rem(t + tiles // 2, tiles)
     send_buf[first] = coefficients(first)
     pl.semaphore_wait(barrier, tiles + 2)
     send(first).start()
 
     @pl.loop(2, tiles)
     def _(i):
-        j = lax.rem(t + i, tiles)
+        j = lax.rem(t + turn(i), tiles)
         send_buf[j] = coefficients(j)
         send(j).start()
 
@@ -204,7 +208,7 @@
         functools.partial(spectra_kernel, tiles),
         out_shape=jax.ShapeDtypeStruct((2, 2, 2, group, half), jnp.bfloat16),
         in_specs=[in_hbm] * 4,
-        out_specs=in_hbm,
+        out_specs=pl.BlockSpec(memory_space=pl.ANY),
         scratch_shapes=[
             pltpu.VMEM((tiles, length, group), jnp.bfloat16),
             pltpu.VMEM((2 * MODES + tiles, length), jnp.float32),
@@ -227,7 +231,7 @@
             pltpu.SemaphoreType.DMA((3,)),
         ],
         compiler_params=pltpu.CompilerParams(
-            collective_id=0, has_side_effects=True, vmem_limit_bytes=60 << 20
+            collective_id=0, has_side_effects=True, vmem_limit_bytes=214 << 18
         ),
     )(records, jnp.asarray(analysis), jnp.asarray(synthesis), channel_live.reshape(1, group))
 
@@ -286,7 +290,7 @@
             pltpu.VMEM((2, group, OFFS, half), jnp.bfloat16),
             pltpu.SemaphoreType.DMA((2, group // CHANNEL_BLOCK)),
         ],
-        compiler_params=pltpu.CompilerParams(vmem_limit_bytes=60 << 20),
+        compiler_params=pltpu.CompilerParams(vmem_limit_bytes=16 << 20),
     )(halves)
 
 

time: 22.2 us -> 21.2 us (0.955)
  Pallas kernels: 22.1 us -> 20.4 us
  local copies, waits for them, and re-layouts: 0 us -> 0.65 us
    pallas_call x1, Pallas kernels: 5.7 us -> 4.76 us  [cross_spectra(): pl.pallas_call(functools.partial(cross_kernel, 1.0 / windows), out_shape=...]
    pallas_call x1, Pallas kernels: 16.4 us -> 15.7 us  [whitened_spectra(): pl.pallas_call(functools.partial(spectra_kernel, tiles), out_shape=jax.Sh...]
    unnamed x0 -> x2, local copies, waits for them, and re-layouts: none -> 0.65 us
where the time goes in v4:
time: 21.2 us; the launch traced here: 21.1 us
  Pallas kernels  20.4 us (96%)
  local copies, waits for them, and re-layouts  0.65 us (3%)
    pallas_call x1, Pallas kernels, whitened_spectra(): pl.pallas_call(functools.partial(spectra_kernel, tiles), out_shape=jax.Sh...  15.7 us
    pallas_call x1, Pallas kernels, cross_spectra(): pl.pallas_call(functools.partial(cross_kernel, 1.0 / windows), out_shape=...  4.76 us
    unnamed x2, local copies, waits for them, and re-layouts  0.65 us

profile of v4, /device:TPU:1, one launch (start us, length us, event | category | flops | bytes accessed | tf_op | source)
XLA Modules:
  0.0 21.1 jit_solution(18004894558931697387)
XLA Ops:
  0.0 0.0 copy-start
  0.0 0.7 %copy-done = s32[128]{0:T(128)S(1)} copy-done((s32[128]{0:T(128)S(1)}, s32[128]{0:T(128)}, u32[]{:S(2)}) %copy-start) | copy-done | bytes 536
  0.7 15.7 %shard_map.46.halves = bf16[2,2,2,128,128]{4,3,2,1,0:T(8,128)(2,1)S(1)} custom-call(bf16[1,1600,1024]{2,1,0:T(8,128)(2,1)} %rec.1, f32[104,1600]{1,0:T(8,128)} %constant.4.clone.analysis, bf16[4,512,192]{2,1,0:T(8,128)(2,1)} %constant.5.clone.synthesis, s32[1,128]{1,0:T(1,128)S(1)} %bitcast.1), custom_call_target="tpu_custom_call" | custom-call | tf_op jit(solution)/shard_map/pallas_call | solution.py:207
  16.3 4.8 %shard_map.47 = bf16[2,128,128,128]{3,2,1,0:T(8,128)(2,1)} custom-call(bf16[2,2,2,128,128]{4,3,2,1,0:T(8,128)(2,1)S(1)} %shard_map.46.halves), custom_call_target="tpu_custom_call" | custom-call | tf_op jit(solution)/shard_map/pallas_call | solution.py:283
Async XLA Ops:
  0.0 0.7 %copy-start = (s32[128]{0:T(128)S(1)}, s32[128]{0:T(128)}, u32[]{:S(2)}) copy-start(s32[128]{0:T(128)} %param.5) | copy-start | bytes 1540
